TPU v7x, 32 devices: a whole 2x2x4 slice. The times are simulated.
32 devices in a mesh: groups: 2 (over x), seq: 8 (over z, y), head: 2 (over core).
Axes of the slice: x: 2, y: 2, z: 4, core: 2. Of those that a mesh axis runs over, the one named last changes fastest.
Arguments:
- query_proj: bfloat16 [4096, 2048], P(('groups', 'seq'), 'head'), parts along dimension 0, may hold values from -6 to 6
- key_proj: bfloat16 [4096, 2048], P(('groups', 'seq'), 'head'), parts along dimension 0, may hold values from -6 to 6
- value_proj: bfloat16 [4096, 2048], P(('groups', 'seq'), 'head'), parts along dimension 0, may hold values from -6 to 6
- segment_ids: int32 [4096], P(('groups', 'seq')), parts along dimension 0, may hold values from 0 to 5, never falling along the last dimension, each value on 1 to 682 neighbouring positions
- feature_map: bfloat16 [16, 128, 256], P('head'), may hold values from -0.5 to 0.5
- head_gain: float32 [2048], P('head'), may hold values from 0.1 to 1.9
- residual: bfloat16 [4096, 2048], P(('groups', 'seq', 'head')), parts along dimension 0, may hold values from -6 to 6
- out_weight: bfloat16 [2048, 2048], P('head'), may hold values from -0.125 to 0.125
- norm_gain: float32 [2048], replicated, may hold values from 0.1 to 1.9
- router: bfloat16 [2048, 16], replicated, may hold values from -0.125 to 0.125
- w_gate: bfloat16 [16, 2048, 1024], P(('seq', 'head')), may hold values from -0.125 to 0.125
- w_up: bfloat16 [16, 2048, 1024], P(('seq', 'head')), may hold values from -0.125 to 0.125
- w_down: bfloat16 [16, 1024, 2048], P(('seq', 'head')), may hold values from -0.1875 to 0.1875
- expert_ids: int32 [4096, 8], P(('groups', 'seq', 'head')), parts along dimension 0, may hold values from 0 to 15, all different within a row; in each aligned block of 128 rows (0 to 127, 128 to 255, ...) at most 80 rows name the same one
Outputs:
- hidden: bfloat16 [4096, 2048], P(('groups', 'seq', 'head')), parts along dimension 0
- expert_sum: bfloat16 [4096, 2048], P(('groups', 'seq', 'head')), parts along dimension 0
There are 2 independent parts, one for each index of `groups`. A program takes and returns all parts, laid end to end along the dimension named above; an argument that names none is the same for every part. Nothing has to cross between parts.
Inputs may be any that keep to these rules, and one draw needn't show every extreme that they name: `segment_ids`: segment ids never fall; every segment has 1 to 682 tokens, one exactly 682. `expert_ids`: A token's 8 experts differ. In the 128 rows of one device (aligned blocks of rows) no expert is named more than 80 times, and in some such block some expert is named exactly 80 times.
All inputs are finite; a program needn't handle non-finite values.
Results may differ from a plain program's by a relative error of at most 0.011.
Values may be sent and summed in bfloat16 or wider, within the bound.
A program may use at most 128 MiB of HBM per device.

v0:
```python
import jax
import jax.numpy as jnp
from jax import lax
from jax.sharding import PartitionSpec as P


def carried_in(last_seg, local_state, token_count):
    place = lax.axis_index("seq")
    blocks = lax.axis_size("seq")
    longest = token_count * blocks // 3
    reach = min(blocks - 1, max(1, (longest - 2) // token_count + 1))
    last_all = lax.all_gather(last_seg, "seq")

    def last_of(back):
        index = place - back
        return jnp.where(index >= 0, last_all[jnp.maximum(index, 0)], -1 - back)

    before = last_of(1)
    carried = None
    window = local_state
    span = 1
    covered = 0
    while covered < reach:
        shifted = lax.ppermute(
            window.astype(jnp.bfloat16), "seq", [(i, i + span) for i in range(blocks - span)]
        ).astype(jnp.float32)
        if carried is None:
            carried = shifted
        else:
            carried = carried + jnp.where(last_of(span) == before, shifted, 0.0)
        covered += span
        if covered < reach:
            window = window + jnp.where(last_of(span) == last_seg, shifted, 0.0)
        span *= 2
    return (before, carried)


def features_of(inputs, feature_map, head_count, head_dim):
    grouped = inputs.reshape(inputs.shape[0], head_count, head_dim)
    projected = jnp.einsum("thd,hdf->thf", grouped, feature_map, preferred_element_type=jnp.float32)
    return (jax.nn.elu(projected) + 1.0).astype(jnp.bfloat16)


def run_expert(rows, gate, w_gate, w_up, w_down):
    gate_pre = jnp.dot(rows, w_gate, preferred_element_type=jnp.float32)
    up_pre = jnp.dot(rows, w_up, preferred_element_type=jnp.float32)
    activated = (jax.nn.silu(gate_pre) * up_pre).astype(jnp.bfloat16)
    answer = jnp.dot(activated, w_down, preferred_element_type=jnp.float32)
    return answer * gate[:, None]


def shards(
    query_proj,
    key_proj,
    value_proj,
    segment_ids,
    feature_map,
    head_gain,
    residual,
    out_weight,
    norm_gain,
    router,
    w_gate,
    w_up,
    w_down,
    expert_ids,
):
    token_count = query_proj.shape[0]
    head_count = feature_map.shape[0]
    head_dim = feature_map.shape[1]
    query_feat = features_of(query_proj, feature_map, head_count, head_dim)
    key_feat = features_of(key_proj, feature_map, head_count, head_dim)
    values = value_proj.reshape(token_count, head_count, head_dim)
    last_seg = segment_ids[token_count - 1]
    tail_mask = (segment_ids == last_seg).astype(jnp.bfloat16)
    local_state = jnp.einsum(
        "thf,thd->hfd",
        key_feat * tail_mask[:, None, None],
        values,
        preferred_element_type=jnp.float32,
    )
    seg_before, state_before = carried_in(last_seg, local_state, token_count)
    scores = jnp.einsum("thf,shf->hts", query_feat, key_feat, preferred_element_type=jnp.float32)
    positions = lax.iota(jnp.int32, token_count)
    allowed = (positions[None, :] <= positions[:, None]) & (
        segment_ids[None, :] == segment_ids[:, None]
    )
    block_weights = jnp.where(allowed[None], scores, 0.0).astype(jnp.bfloat16)
    within = jnp.einsum("hts,shd->thd", block_weights, values, preferred_element_type=jnp.float32)
    carried = jnp.einsum(
        "thf,hfd->thd",
        query_feat,
        state_before.astype(jnp.bfloat16),
        preferred_element_type=jnp.float32,
    )
    carry_mask = (segment_ids == seg_before).astype(jnp.float32)
    mixed = within + carry_mask[:, None, None] * carried
    scale = lax.rsqrt(jnp.mean(mixed * mixed, axis=2, keepdims=True) + 1e-06)
    attn_heads = (
        (mixed * scale * head_gain.reshape(head_count, head_dim))
        .reshape(token_count, head_count * head_dim)
        .astype(jnp.bfloat16)
    )
    attn_rows = lax.all_to_all(attn_heads, "head", split_axis=0, concat_axis=1, tiled=True)
    projected = jnp.dot(
        attn_rows,
        lax.all_gather(out_weight, "head", axis=0, tiled=True),
        preferred_element_type=jnp.float32,
    )
    hidden = (residual.astype(jnp.float32) + projected).astype(jnp.bfloat16)
    hidden_f = hidden.astype(jnp.float32)
    normed = (
        hidden_f
        * lax.rsqrt(jnp.mean(hidden_f * hidden_f, axis=1, keepdims=True) + 1e-05)
        * norm_gain
    ).astype(jnp.bfloat16)
    logits = jnp.dot(normed, router, preferred_element_type=jnp.float32)
    expert_count = router.shape[1]
    expert_iota = lax.iota(jnp.int32, expert_count)
    picked = expert_ids[:, :, None] == expert_iota[None, None, :]
    chosen = jnp.sum(jnp.where(picked, logits[:, None, :], 0.0), axis=2)
    gates = jax.nn.sigmoid(chosen)
    gate_weights = gates / jnp.sum(gates, axis=1, keepdims=True)
    dense_gates = jnp.sum(jnp.where(picked, gate_weights[:, :, None], 0.0), axis=1)
    spread = ("seq", "head")
    all_rows = lax.all_gather(normed, spread, axis=0, tiled=True)
    all_gates = lax.all_gather(dense_gates, spread, axis=0, tiled=True)
    exp_dev = w_gate.shape[0]
    first = (lax.axis_index("seq") * lax.axis_size("head") + lax.axis_index("head")) * exp_dev
    partial = 0.0
    for own in range(exp_dev):
        gate = jnp.sum(jnp.where(expert_iota[None, :] == first + own, all_gates, 0.0), axis=1)
        partial = partial + run_expert(all_rows, gate, w_gate[own], w_up[own], w_down[own])
    expert_sum = lax.psum_scatter(
        partial.astype(jnp.bfloat16), spread, scatter_dimension=0, tiled=True
    )
    return (hidden, expert_sum)


def solution(mesh):
    placed = (
        P(("groups", "seq"), "head"),
        P(("groups", "seq"), "head"),
        P(("groups", "seq"), "head"),
        P(("groups", "seq")),
        P("head", None, None),
        P("head"),
        P(("groups", "seq", "head"), None),
        P("head", None),
        P(),
        P(),
        P(("seq", "head"), None, None),
        P(("seq", "head"), None, None),
        P(("seq", "head"), None, None),
        P(("groups", "seq", "head"), None),
    )
    return jax.shard_map(
        shards,
        mesh=mesh,
        in_specs=placed,
        out_specs=(P(("groups", "seq", "head"), None), P(("groups", "seq", "head"), None)),
        check_vma=False,
    )
```

profile of v0, /device:TPU:0, one launch (start us, length us, event | category | flops | bytes accessed | tf_op | source)
XLA Modules:
  0.0 290.1 jit_solution(12551976899202699490)
XLA Ops:
  7.3 0.7 all-gather.3.cloned.1.call-update
  8.6 1.2 slice_dynamic-update-slice_fusion
  9.9 13.1 %all-reduce = s32[8]{0:T(128)S(1)} all-reduce(s32[8]{0:T(128)S(1)} %get-tuple-element.4), channel_id=1, replica_groups=mesh['groups'=2,'seq'=8,'head'=2] {'seq'}, use_global_device_ids=true, to_apply=%add | all-reduce | flops 8 | bytes 64
  22.9 0.6 fusion.43
  24.2 0.7 compare_convert_fusion.1
  24.9 1.1 fusion.12
  26.1 1.2 fusion.44
  27.3 3.4 %collective-permute-start = (bf16[8,256,128]{2,1,0:T(8,128)(2,1)}, bf16[8,256,128]{2,1,0:T(8,128)(2,1)S(1)}, u32[]{:S(2)}, u32[]{:S(2)}) collective-permute-start(bf16[8,256,128]{2,1,0:T(8,128)(2,1)} %get-tuple-element.8), channel_id=1, source_target_pairs={{0,2},{2,4},{4,6},{6,8},{8,10},{10,12},{12,14},{1,3},{3,5},{5,7},{... | collective-permute-start | bytes 1572872 | tf_op jit(solution)/shard_map/ppermute | solution.py:24
  31.4 7.9 %collective-permute-done = bf16[8,256,128]{2,1,0:T(8,128)(2,1)S(1)} collective-permute-done((bf16[8,256,128]{2,1,0:T(8,128)(2,1)}, bf16[8,256,128]{2,1,0:T(8,128)(2,1)S(1)}, u32[]{:S(2)}, u32[]{:S(2)}) %collective-permute-start) | collective-permute-done | bytes 524320 | tf_op jit(solution)/shard_map/ppermute | solution.py:24
  39.3 0.9 fusion.18
  40.2 4.4 %collective-permute-start.1 = (bf16[8,256,128]{2,1,0:T(8,128)(2,1)}, bf16[8,256,128]{2,1,0:T(8,128)(2,1)S(1)}, u32[]{:S(2)}, u32[]{:S(2)}) collective-permute-start(bf16[8,256,128]{2,1,0:T(8,128)(2,1)} %fusion.18), channel_id=1, source_target_pairs={{0,4},{2,6},{4,8},{6,10},{8,12},{10,14},{1,5},{3,7},{5,9},{7,11},{... | collective-permute-start | bytes 1572872 | tf_op jit(solution)/shard_map/ppermute | solution.py:24
  45.4 2.2 fusion.9
  47.6 5.0 %collective-permute-done.1 = bf16[8,256,128]{2,1,0:T(8,128)(2,1)S(1)} collective-permute-done((bf16[8,256,128]{2,1,0:T(8,128)(2,1)}, bf16[8,256,128]{2,1,0:T(8,128)(2,1)S(1)}, u32[]{:S(2)}, u32[]{:S(2)}) %collective-permute-start.1) | collective-permute-done | bytes 524320 | tf_op jit(solution)/shard_map/ppermute | solution.py:24
  52.6 1.4 fusion.16
  54.0 2.5 multiply_reduce_fusion
  57.0 4.2 %all_to_all.16 = bf16[2,128,1024]{1,2,0:T(8,128)(2,1)S(1)} all-to-all(bf16[2,128,1024]{1,2,0:T(8,128)(2,1)S(1)} %copy.47), channel_id=1, replica_groups=mesh['groups'=2,'seq'=8,'head'=2] {'head'}, dimensions={0} | all-to-all | bytes 1048576 | tf_op jit(solution)/shard_map/all_to_all | solution.py:104
  61.2 4.8 %fusion.20 = (f32[128]{0:T(128)S(1)}, bf16[128,2048]{1,0:T(8,128)(2,1)S(1)}) fusion(bf16[128,2048]{0,1:T(8,128)(2,1)S(1)} %bitcast.71, bf16[2048,2048]{1,0:T(8,128)(2,1)} %all-gather.3.cloned.1.call-done, bf16[128,2048]{1,0:T(8,128)(2,1)S(1)} %copy-done.3), kind=kOutput, calls=%fused_computation.32 | convolution fusion | flops 1075314560 | bytes 9961984 | tf_op jit(solution)/shard_map/dot_general | solution.py:105
  66.0 1.0 fusion.22
  67.1 1.3 fusion.45
  68.5 20.6 %all_gather.15 = f32[2048,16]{0,1:T(8,128)S(1)} all-gather(f32[128,16]{0,1:T(8,128)S(1)} %select_reduce_fusion.1), channel_id=1, replica_groups=mesh['groups'=2,'seq'=8,'head'=2] {'seq','head'}, dimensions={0}, use_global_device_ids=true | all-gather | bytes 139264 | tf_op jit(solution)/shard_map/all_gather | solution.py:127
  89.2 51.7 %all-gather.5.cloned.1.call-done = bf16[2048,2048]{1,0:T(8,128)(2,1)} async-done(((bf16[128,2048]{1,0:T(8,128)(2,1)}), bf16[2048,2048]{1,0:T(8,128)(2,1)}) %all-gather.5.cloned.1.call-update) | async-done | bytes 8388624 | tf_op jit(solution)/shard_map/all_gather | solution.py:126
  140.9 14.4 %fusion.3 = f32[2048,1024]{1,0:T(8,128)} fusion(bf16[2048,2048]{1,0:T(8,128)(2,1)} %all-gather.5.cloned.1.call-done, bf16[1,2048,1024]{2,1,0:T(8,128)(2,1)} %param.24), kind=kOutput, calls=%fused_computation.8 | convolution fusion | flops 8589934592 | bytes 20971520 | tf_op jit(solution)/shard_map/dot_general | solution.py:45
  155.3 26.0 %multiply_convert_fusion = bf16[2048,2048]{1,0:T(8,128)(2,1)} fusion(f32[2048]{0:T(1024)S(1)} %select_reduce_fusion, f32[2048,1024]{1,0:T(8,128)} %fusion.3, bf16[2048,2048]{1,0:T(8,128)(2,1)} %all-gather.5.cloned.1.call-done, bf16[1,1024,2048]{2,1,0:T(8,128)(2,1)} %param.26, bf16[1,2048,1024]{2,1,0:T(8,128)(2,1)} %param.25), kind=kOutput, calls=%fused_computation | convolution fusion | flops 17200840704 | bytes 33562624 | tf_op jit(solution)/shard_map/dot_general | solution.py:48
  181.3 102.2 %reduce-scatter.2.cloned.1.call-done = bf16[128,2048]{1,0:T(8,128)(2,1)} async-done(((bf16[2048,2048]{1,0:T(8,128)(2,1)}), bf16[128,2048]{1,0:T(8,128)(2,1)}) %reduce-scatter.2.cloned.1.call-update) | async-done | bytes 524304 | tf_op jit(solution)/shard_map/reduce_scatter | solution.py:134
  (44 shorter events, 1.5 us)
Async XLA Ops:
  7.2 17.7 %copy-start = (bf16[8,128,256]{2,1,0:T(8,128)(2,1)S(1)}, bf16[8,128,256]{2,1,0:T(8,128)(2,1)}, u32[]{:S(2)}) copy-start(bf16[8,128,256]{2,1,0:T(8,128)(2,1)} %param.18) | copy-start | bytes 1572868
  7.2 0.8 copy-start.11
  7.2 1.4 copy-start.7
  7.2 17.7 %copy-start.10 = (bf16[256,1024]{1,0:T(8,128)(2,1)S(1)}, bf16[256,1024]{1,0:T(8,128)(2,1)}, u32[]{:S(2)}) copy-start(bf16[256,1024]{1,0:T(8,128)(2,1)} %param.15) | copy-start | bytes 1572868
  7.2 18.8 %copy-start.4 = (bf16[256,1024]{1,0:T(8,128)(2,1)S(1)}, bf16[256,1024]{1,0:T(8,128)(2,1)}, u32[]{:S(2)}) copy-start(bf16[256,1024]{1,0:T(8,128)(2,1)} %param.16) | copy-start | bytes 1572868
  7.2 53.9 %all-gather.3.cloned.1.call-start = ((), (), s32[]{:S(2)}) async-start(), calls=%async_computation.2 | async-start | bytes 12582912 | tf_op jit(solution)/shard_map/all_gather | solution.py:107
  8.0 133.0 %all-gather.5.cloned.1.call-start = ((), (), s32[]{:S(2)}) async-start(), calls=%async_computation.3 | async-start | bytes 8912896 | tf_op jit(solution)/shard_map/all_gather | solution.py:126
  27.3 12.0 %collective-permute-start = (bf16[8,256,128]{2,1,0:T(8,128)(2,1)}, bf16[8,256,128]{2,1,0:T(8,128)(2,1)S(1)}, u32[]{:S(2)}, u32[]{:S(2)}) collective-permute-start(bf16[8,256,128]{2,1,0:T(8,128)(2,1)} %get-tuple-element.8), channel_id=1, source_target_pairs={{0,2},{2,4},{4,6},{6,8},{8,10},{10,12},{12,14},{1,3},{3,5},{5,7},{... | collective-permute-start | bytes 1572872 | tf_op jit(solution)/shard_map/ppermute | solution.py:24
  40.2 12.3 %collective-permute-start.1 = (bf16[8,256,128]{2,1,0:T(8,128)(2,1)}, bf16[8,256,128]{2,1,0:T(8,128)(2,1)S(1)}, u32[]{:S(2)}, u32[]{:S(2)}) collective-permute-start(bf16[8,256,128]{2,1,0:T(8,128)(2,1)} %fusion.18), channel_id=1, source_target_pairs={{0,4},{2,6},{4,8},{6,10},{8,12},{10,14},{1,5},{3,7},{5,9},{7,11},{... | collective-permute-start | bytes 1572872 | tf_op jit(solution)/shard_map/ppermute | solution.py:24
  47.5 5.0 %copy-start.2 = (bf16[256,8,256]{0,2,1:T(8,128)(2,1)}, bf16[256,8,256]{0,2,1:T(8,128)(2,1)S(1)}, u32[]{:S(2)}) copy-start(bf16[256,8,256]{0,2,1:T(8,128)(2,1)S(1)} %fusion.9) | copy-start | bytes 3145732
  47.5 9.0 %copy-start.9 = (f32[1024]{0:T(1024)S(1)}, f32[1024]{0:T(1024)}, u32[]{:S(2)}) copy-start(f32[1024]{0:T(1024)} %param.19) | copy-start | bytes 12292
  54.0 7.1 %copy-start.3 = (bf16[128,2048]{1,0:T(8,128)(2,1)S(1)}, bf16[128,2048]{1,0:T(8,128)(2,1)}, u32[]{:S(2)}) copy-start(bf16[128,2048]{1,0:T(8,128)(2,1)} %param.20) | copy-start | bytes 1572868
  61.1 4.9 %copy-start.8 = (f32[2048]{0:T(1024)S(1)}, f32[2048]{0:T(1024)}, u32[]{:S(2)}) copy-start(f32[2048]{0:T(1024)} %param.22) | copy-start | bytes 24580
  61.1 5.9 %copy-start.5 = (bf16[2048,16]{0,1:T(8,128)(2,1)S(1)}, bf16[2048,16]{0,1:T(8,128)(2,1)}, u32[]{:S(2)}) copy-start(bf16[2048,16]{0,1:T(8,128)(2,1)} %param.23) | copy-start | bytes 196612
  61.1 7.2 %copy-start.6 = (s32[128,8]{0,1:T(8,128)S(1)}, s32[128,8]{0,1:T(8,128)}, u32[]{:S(2)}) copy-start(s32[128,8]{0,1:T(8,128)} %param.27) | copy-start | bytes 12292
  66.0 89.4 %copy-start.1 = (bf16[128,2048]{1,0:T(8,128)(2,1)}, bf16[128,2048]{1,0:T(8,128)(2,1)S(1)}, u32[]{:S(2)}) copy-start(bf16[128,2048]{1,0:T(8,128)(2,1)S(1)} %get-tuple-element.13) | copy-start | bytes 1572868
  67.0 216.5 %reduce-scatter.2.cloned.1.call-start = ((), (), s32[]{:S(2)}) async-start(), calls=%async_computation.4 | async-start | bytes 8912896 | tf_op jit(solution)/shard_map/reduce_scatter | solution.py:134
Sparse Core Ops, SparseCore 0:
  9.6 22.5 all-gather.2
  67.1 73.7 all-gather.4
  181.5 102.0 reduce-scatter.1
where the time goes:
time: 290 us
  waiting for transfers between devices  168 us (58%)
  matrix products  54.9 us (19%)
  blocking collectives  37.9 us (13%)
  between operations  16 us (6%)
  starting transfers between devices  7.95 us (3%)
  other arithmetic  3.09 us (1%)
    reduce_scatter x1, waiting for transfers between devices, shards(): lax.psum_scatter(partial.astype(jnp.bfloat16), spread, scatter_dimension=...  102 us
    all_gather x1, waiting for transfers between devices, shards(): all_rows = lax.all_gather(normed, spread, axis=0, tiled=True)  51.7 us
    dot_general x1, matrix products, run_expert(): answer = jnp.dot(activated, w_down, preferred_element_type=jnp.float32)  26 us
    all_gather x1, blocking collectives, shards(): all_gates = lax.all_gather(dense_gates, spread, axis=0, tiled=True)  20.6 us
    dot_general x1, matrix products, run_expert(): gate_pre = jnp.dot(rows, w_gate, preferred_element_type=jnp.float32)  14.4 us
    unnamed x1, blocking collectives  13.1 us
    ppermute x2, waiting for transfers between devices, carried_in(): lax.ppermute(window.astype(jnp.bfloat16), 'seq', [(i, i + span) for i in...  12.9 us
    ppermute x2, starting transfers between devices, carried_in(): lax.ppermute(window.astype(jnp.bfloat16), 'seq', [(i, i + span) for i in...  7.83 us
  transfers between devices with their start and end apart: 5, of which 4 were waited for; matrix products, arithmetic and copies ran while one was open for 5% of the time, Pallas kernels for 0%

commit v1 on v0

--- a/solution.py
+++ b/solution.py
@@ -123,8 +123,14 @@
     gate_weights = gates / jnp.sum(gates, axis=1, keepdims=True)
     dense_gates = jnp.sum(jnp.where(picked, gate_weights[:, :, None], 0.0), axis=1)
     spread = ("seq", "head")
-    all_rows = lax.all_gather(normed, spread, axis=0, tiled=True)
-    all_gates = lax.all_gather(dense_gates, spread, axis=0, tiled=True)
+    carry_desk = lambda my_tile, xs, comm_axis: jnp.split(
+        jax.lax.all_gather(
+            jnp.concatenate([my_tile, xs], 1), axis_name=comm_axis, axis=0, tiled=True
+        ),
+        [my_tile.shape[1]],
+        1,
+    )
+    all_rows, all_gates = carry_desk(normed, dense_gates, spread)
     exp_dev = w_gate.shape[0]
     first = (lax.axis_index("seq") * lax.axis_size("head") + lax.axis_index("head")) * exp_dev
     partial = 0.0

time: 290 us -> 315 us (1.086)
  waiting for transfers between devices: 168 us -> 210 us
  blocking collectives: 37.9 us -> 17.2 us
    all_gather x1, waiting for transfers between devices: 51.7 us -> 93 us  [shards(): jax.lax.all_gather(jnp.concatenate([my_tile, xs], 1), axis_name=comm_axis...]
    all_gather x1 -> x0, blocking collectives: 20.6 us -> none  [shards(): all_gates = lax.all_gather(dense_gates, spread, axis=0, tiled=True)]
  transfers between devices with their start and end apart: 5 -> 5, of which waited for: 4 -> 4; matrix products, arithmetic and copies ran while one was open for 5% -> 4% of each run, Pallas kernels for 0% -> 0%
where the time goes in v1:
time: 315 us; the launch traced here: 314 us
  waiting for transfers between devices  210 us (67%)
  matrix products  55 us (17%)
  blocking collectives  17.2 us (5%)
  between operations  16 us (5%)
  starting transfers between devices  8.13 us (3%)
  other arithmetic  4.86 us (2%)
    reduce_scatter x1, waiting for transfers between devices, shards(): lax.psum_scatter(partial.astype(jnp.bfloat16), spread, scatter_dimension=...  104 us
    all_gather x1, waiting for transfers between devices, shards(): jax.lax.all_gather(jnp.concatenate([my_tile, xs], 1), axis_name=comm_axis...  93 us
    dot_general x1, matrix products, run_expert(): answer = jnp.dot(activated, w_down, preferred_element_type=jnp.float32)  25.9 us
    dot_general x1, matrix products, run_expert(): gate_pre = jnp.dot(rows, w_gate, preferred_element_type=jnp.float32)  15.6 us
    unnamed x1, blocking collectives  13.1 us
    ppermute x2, waiting for transfers between devices, carried_in(): lax.ppermute(window.astype(jnp.bfloat16), 'seq', [(i, i + span) for i in...  12.9 us
    ppermute x2, starting transfers between devices, carried_in(): lax.ppermute(window.astype(jnp.bfloat16), 'seq', [(i, i + span) for i in...  7.83 us
  transfers between devices with their start and end apart: 5, of which 4 were waited for; matrix products, arithmetic and copies ran while one was open for 4% of the time, Pallas kernels for 0%

profile of v1, /device:TPU:0, one launch (start us, length us, event | category | flops | bytes accessed | tf_op | source)
XLA Modules:
  0.0 314.3 jit_solution(13112510402077097500)
XLA Ops:
  7.3 0.7 all-gather.3.cloned.1.call-update
  8.0 0.6 dynamic-slice
  8.6 1.2 slice_dynamic-update-slice_fusion
  9.9 13.1 %all-reduce = s32[8]{0:T(128)S(1)} all-reduce(s32[8]{0:T(128)S(1)} %get-tuple-element.4), channel_id=1, replica_groups=mesh['groups'=2,'seq'=8,'head'=2] {'seq'}, use_global_device_ids=true, to_apply=%add | all-reduce | flops 8 | bytes 64
  22.9 0.6 fusion.54
  24.2 0.7 compare_convert_fusion.1
  24.9 1.1 fusion.19
  26.0 1.2 fusion.55
  27.2 3.4 %collective-permute-start = (bf16[8,256,128]{2,1,0:T(8,128)(2,1)}, bf16[8,256,128]{2,1,0:T(8,128)(2,1)S(1)}, u32[]{:S(2)}, u32[]{:S(2)}) collective-permute-start(bf16[8,256,128]{2,1,0:T(8,128)(2,1)} %get-tuple-element.8), channel_id=1, source_target_pairs={{0,2},{2,4},{4,6},{6,8},{8,10},{10,12},{12,14},{1,3},{3,5},{5,7},{... | collective-permute-start | bytes 1572872 | tf_op jit(solution)/shard_map/ppermute | solution.py:24
  31.4 7.9 %collective-permute-done = bf16[8,256,128]{2,1,0:T(8,128)(2,1)S(1)} collective-permute-done((bf16[8,256,128]{2,1,0:T(8,128)(2,1)}, bf16[8,256,128]{2,1,0:T(8,128)(2,1)S(1)}, u32[]{:S(2)}, u32[]{:S(2)}) %collective-permute-start) | collective-permute-done | bytes 524320 | tf_op jit(solution)/shard_map/ppermute | solution.py:24
  39.3 0.9 fusion.25
  40.2 4.4 %collective-permute-start.1 = (bf16[8,256,128]{2,1,0:T(8,128)(2,1)}, bf16[8,256,128]{2,1,0:T(8,128)(2,1)S(1)}, u32[]{:S(2)}, u32[]{:S(2)}) collective-permute-start(bf16[8,256,128]{2,1,0:T(8,128)(2,1)} %fusion.25), channel_id=1, source_target_pairs={{0,4},{2,6},{4,8},{6,10},{8,12},{10,14},{1,5},{3,7},{5,9},{7,11},{... | collective-permute-start | bytes 1572872 | tf_op jit(solution)/shard_map/ppermute | solution.py:24
  45.3 2.2 fusion.16
  47.5 5.0 %collective-permute-done.1 = bf16[8,256,128]{2,1,0:T(8,128)(2,1)S(1)} collective-permute-done((bf16[8,256,128]{2,1,0:T(8,128)(2,1)}, bf16[8,256,128]{2,1,0:T(8,128)(2,1)S(1)}, u32[]{:S(2)}, u32[]{:S(2)}) %collective-permute-start.1) | collective-permute-done | bytes 524320 | tf_op jit(solution)/shard_map/ppermute | solution.py:24
  52.5 1.4 fusion.23
  54.0 2.5 multiply_reduce_fusion
  56.9 4.2 %all_to_all.16 = bf16[2,128,1024]{1,2,0:T(8,128)(2,1)S(1)} all-to-all(bf16[2,128,1024]{1,2,0:T(8,128)(2,1)S(1)} %copy.47), channel_id=1, replica_groups=mesh['groups'=2,'seq'=8,'head'=2] {'head'}, dimensions={0} | all-to-all | bytes 1048576 | tf_op jit(solution)/shard_map/all_to_all | solution.py:104
  61.1 4.8 %fusion.27 = (f32[128]{0:T(128)S(1)}, bf16[128,2048]{1,0:T(8,128)(2,1)S(1)}) fusion(bf16[128,2048]{0,1:T(8,128)(2,1)S(1)} %bitcast.68, bf16[2048,2048]{1,0:T(8,128)(2,1)} %all-gather.3.cloned.1.call-done, bf16[128,2048]{1,0:T(8,128)(2,1)S(1)} %copy-done.4), kind=kOutput, calls=%fused_computation.36 | convolution fusion | flops 1075314560 | bytes 9961984 | tf_op jit(solution)/shard_map/dot_general | solution.py:105
  66.7 1.1 pad_maximum_fusion
  68.1 93.0 %all-gather.5.cloned.1.call-done = f32[2048,2064]{1,0:T(8,128)} async-done(((f32[128,2064]{1,0:T(8,128)}), f32[2048,2064]{1,0:T(8,128)}) %all-gather.5.cloned.1.call-update) | async-done | bytes 16908304 | tf_op jit(solution)/shard_map/all_gather | solution.py:127
  161.0 1.6 fusion.30
  162.6 15.6 %fusion.2 = f32[2048,1024]{1,0:T(8,128)} fusion(f32[2048,2064]{1,0:T(8,128)} %all-gather.5.cloned.1.call-done, bf16[1,2048,1024]{2,1,0:T(8,128)(2,1)} %param.24), kind=kOutput, calls=%fused_computation.3 | convolution fusion | flops 8589934592 | bytes 20971520 | tf_op jit(solution)/shard_map/dot_general | solution.py:45
  178.2 25.9 %multiply_convert_fusion = bf16[2048,2048]{1,0:T(8,128)(2,1)} fusion(f32[2048]{0:T(1024)S(1)} %fusion.30, f32[2048,1024]{1,0:T(8,128)} %fusion.2, f32[2048,2064]{1,0:T(8,128)} %all-gather.5.cloned.1.call-done, bf16[1,1024,2048]{2,1,0:T(8,128)(2,1)} %param.26, bf16[1,2048,1024]{2,1,0:T(8,128)(2,1)} %param.25), kind=kOutput, calls=%fused_computation | convolution fusion | flops 17200840704 | bytes 33562624 | tf_op jit(solution)/shard_map/dot_general | solution.py:48
  204.1 103.6 %reduce-scatter.2.cloned.1.call-done = bf16[128,2048]{1,0:T(8,128)(2,1)} async-done(((bf16[2048,2048]{1,0:T(8,128)(2,1)}), bf16[128,2048]{1,0:T(8,128)(2,1)}) %reduce-scatter.2.cloned.1.call-update) | async-done | bytes 524304 | tf_op jit(solution)/shard_map/reduce_scatter | solution.py:140
  (47 shorter events, 1.6 us)
Async XLA Ops:
  7.2 17.7 %copy-start = (bf16[8,128,256]{2,1,0:T(8,128)(2,1)S(1)}, bf16[8,128,256]{2,1,0:T(8,128)(2,1)}, u32[]{:S(2)}) copy-start(bf16[8,128,256]{2,1,0:T(8,128)(2,1)} %param.18) | copy-start | bytes 1572868
  7.2 0.8 copy-start.12
  7.2 1.4 copy-start.7
  7.2 17.7 %copy-start.10 = (bf16[256,1024]{1,0:T(8,128)(2,1)S(1)}, bf16[256,1024]{1,0:T(8,128)(2,1)}, u32[]{:S(2)}) copy-start(bf16[256,1024]{1,0:T(8,128)(2,1)} %param.15) | copy-start | bytes 1572868
  7.2 18.8 %copy-start.5 = (bf16[256,1024]{1,0:T(8,128)(2,1)S(1)}, bf16[256,1024]{1,0:T(8,128)(2,1)}, u32[]{:S(2)}) copy-start(bf16[256,1024]{1,0:T(8,128)(2,1)} %param.16) | copy-start | bytes 1572868
  7.2 53.9 %all-gather.3.cloned.1.call-start = ((), (), s32[]{:S(2)}) async-start(), calls=%async_computation.2 | async-start | bytes 12582912 | tf_op jit(solution)/shard_map/all_gather | solution.py:107
  8.0 153.1 %all-gather.5.cloned.1.call-start = ((), (), s32[]{:S(2)}) async-start(), calls=%async_computation.3 | async-start | bytes 18939904 | tf_op jit(solution)/shard_map/all_gather | solution.py:127
  27.2 12.0 %collective-permute-start = (bf16[8,256,128]{2,1,0:T(8,128)(2,1)}, bf16[8,256,128]{2,1,0:T(8,128)(2,1)S(1)}, u32[]{:S(2)}, u32[]{:S(2)}) collective-permute-start(bf16[8,256,128]{2,1,0:T(8,128)(2,1)} %get-tuple-element.8), channel_id=1, source_target_pairs={{0,2},{2,4},{4,6},{6,8},{8,10},{10,12},{12,14},{1,3},{3,5},{5,7},{... | collective-permute-start | bytes 1572872 | tf_op jit(solution)/shard_map/ppermute | solution.py:24
  40.2 12.3 %collective-permute-start.1 = (bf16[8,256,128]{2,1,0:T(8,128)(2,1)}, bf16[8,256,128]{2,1,0:T(8,128)(2,1)S(1)}, u32[]{:S(2)}, u32[]{:S(2)}) collective-permute-start(bf16[8,256,128]{2,1,0:T(8,128)(2,1)} %fusion.25), channel_id=1, source_target_pairs={{0,4},{2,6},{4,8},{6,10},{8,12},{10,14},{1,5},{3,7},{5,9},{7,11},{... | collective-permute-start | bytes 1572872 | tf_op jit(solution)/shard_map/ppermute | solution.py:24
  47.5 5.0 %copy-start.3 = (bf16[256,8,256]{0,2,1:T(8,128)(2,1)}, bf16[256,8,256]{0,2,1:T(8,128)(2,1)S(1)}, u32[]{:S(2)}) copy-start(bf16[256,8,256]{0,2,1:T(8,128)(2,1)S(1)} %fusion.16) | copy-start | bytes 3145732
  47.5 9.0 %copy-start.9 = (f32[1024]{0:T(1024)S(1)}, f32[1024]{0:T(1024)}, u32[]{:S(2)}) copy-start(f32[1024]{0:T(1024)} %param.19) | copy-start | bytes 12292
  54.0 7.1 %copy-start.4 = (bf16[128,2048]{1,0:T(8,128)(2,1)S(1)}, bf16[128,2048]{1,0:T(8,128)(2,1)}, u32[]{:S(2)}) copy-start(bf16[128,2048]{1,0:T(8,128)(2,1)} %param.20) | copy-start | bytes 1572868
  61.1 4.8 %copy-start.8 = (f32[2048]{0:T(1024)S(1)}, f32[2048]{0:T(1024)}, u32[]{:S(2)}) copy-start(f32[2048]{0:T(1024)} %param.22) | copy-start | bytes 24580
  61.1 5.0 %copy-start.11 = (bf16[2048,16]{0,1:T(8,128)(2,1)S(1)}, bf16[2048,16]{0,1:T(8,128)(2,1)}, u32[]{:S(2)}) copy-start(bf16[2048,16]{0,1:T(8,128)(2,1)} %param.23) | copy-start | bytes 196612
  61.1 5.4 %copy-start.6 = (s32[128,8]{0,1:T(8,128)S(1)}, s32[128,8]{0,1:T(8,128)}, u32[]{:S(2)}) copy-start(s32[128,8]{0,1:T(8,128)} %param.27) | copy-start | bytes 12292
  65.9 112.3 %copy-start.2 = (bf16[128,2048]{1,0:T(8,128)(2,1)}, bf16[128,2048]{1,0:T(8,128)(2,1)S(1)}, u32[]{:S(2)}) copy-start(bf16[128,2048]{1,0:T(8,128)(2,1)S(1)} %get-tuple-element.13) | copy-start | bytes 1572868
  67.8 239.9 %reduce-scatter.2.cloned.1.call-start = ((), (), s32[]{:S(2)}) async-start(), calls=%async_computation.4 | async-start | bytes 8912896 | tf_op jit(solution)/shard_map/reduce_scatter | solution.py:140
  204.1 103.6 %copy-start.1 = (bf16[8,128,256]{2,1,0:T(8,128)(2,1)S(1)}, bf16[8,128,256]{2,1,0:T(8,128)(2,1)}, u32[]{:S(2)}) copy-start(bf16[8,128,256]{2,1,0:T(8,128)(2,1)} %param.18) | copy-start | bytes 1572868
Sparse Core Ops, SparseCore 0:
  9.6 22.5 all-gather.2
  67.9 93.0 all-gather.4
  204.2 103.4 reduce-scatter.1
